TPU v7x, 256 devices: a whole 4x4x8 slice. The times are simulated.
256 devices in a mesh: gx: 8 (over x, core), gy: 32 (over z, y).
Axes of the slice: x: 4, y: 4, z: 8, core: 2. Of those that a mesh axis runs over, the one named last changes fastest.
Arguments:
- source: bfloat16 [16, 4096, 256], P(None, ('gx', 'gy')), may hold values from -6 to 6
- leaf_flux: bfloat16 [262144, 256], P(('gx', 'gy')), may hold values from -0.375 to 0.375
- leaf_particular: bfloat16 [1048576, 256], P(('gx', 'gy')), may hold values from -0.375 to 0.375
- leaf_lift: bfloat16 [262144, 256], P(('gx', 'gy')), may hold values from -0.75 to 0.75
- box_up: bfloat16 [163840, 1024], P(('gx', 'gy')), may hold values from -0.1875 to 0.1875
- box_down: bfloat16 [262144, 640], P(('gx', 'gy')), may hold values from -0.25 to 0.25
- up_one: bfloat16 [65536, 768], P(('gx', 'gy')), may hold values from -0.1875 to 0.1875
- down_one: bfloat16 [65536, 768], P(('gx', 'gy')), may hold values from -0.21875 to 0.21875
- up_two: bfloat16 [32768, 1536], P(('gx', 'gy')), may hold values from -0.125 to 0.125
- down_two: bfloat16 [32768, 1536], P(('gx', 'gy')), may hold values from -0.15625 to 0.15625
- up_root: bfloat16 [16384, 6144], P(('gx', 'gy')), may hold values from -0.046875 to 0.046875
- down_root: bfloat16 [16384, 6144], P(('gx', 'gy')), may hold values from -0.078125 to 0.078125
Outputs:
- solution: float32 [16, 4096, 256], P(None, ('gx', 'gy'))
All inputs are finite; a program needn't handle non-finite values.
Results may differ from a plain program's by a relative error of at most 0.014.
Values may be sent and summed in bfloat16 or wider, within the bound.
A program may use at most 64 MiB of HBM per device.

v0:
```python
import jax
import jax.numpy as jnp
from jax import lax
from jax.sharding import PartitionSpec as P


def partner(x, axis, stride):
    return lax.ppermute(x, axis, [(i, i ^ 1 << stride) for i in range(lax.axis_size(axis))])


def contract(left, right):
    return lax.dot_general(
        left, right, (((1,), (1,)), ((), ())), preferred_element_type=jnp.float32
    )


def place_pair(joined, other, place, bit_num):
    upper = place // 2**bit_num % 2 == 1
    lower = jnp.where(upper, other, joined)
    higher = jnp.where(upper, joined, other)
    return jnp.concatenate([lower, higher], axis=1)


def sum_sixteen(term):
    total = term
    for bit_num in range(4):
        total = total + partner(total.astype(jnp.bfloat16), ("gx", "gy"), bit_num).astype(
            total.dtype
        )
    return total


def join_sixteen(piece, place):
    joined = piece
    for bit_num in range(4):
        other = partner(joined, ("gx", "gy"), bit_num)
        joined = place_pair(joined, other, place, bit_num)
    return joined


def per_device(
    source,
    leaf_flux,
    leaf_particular,
    leaf_lift,
    box_up,
    box_down,
    up_one,
    down_one,
    up_two,
    down_two,
    up_root,
    down_root,
):
    rhs_count, leaves, points = source.shape
    edge_count = leaf_flux.shape[0] // leaves
    rows_count = lax.axis_size("gy")
    row_place = lax.axis_index("gy")
    place = lax.axis_index("gx") * rows_count + row_place
    k_zero = up_one.shape[0]
    inner_dev = box_up.shape[0] - k_zero
    second_width = up_two.shape[0]
    root_width = up_root.shape[0]
    flux = jnp.einsum(
        "rlq,leq->rle",
        source,
        leaf_flux.reshape(leaves, edge_count, points),
        preferred_element_type=jnp.float32,
    )
    flux = flux.astype(jnp.bfloat16).reshape(rhs_count, leaves * edge_count)
    box_state = contract(flux, box_up).astype(jnp.bfloat16)
    first_term = jnp.dot(box_state[:, inner_dev:], up_one, preferred_element_type=jnp.float32)
    first_sum = first_term
    for bit_num in range(2):
        first_sum = first_sum + partner(first_sum.astype(jnp.bfloat16), "gy", bit_num).astype(
            first_sum.dtype
        )
    first_state = first_sum.astype(jnp.bfloat16)
    k_one = first_state.shape[1] - k_zero
    second_piece = lax.dynamic_slice_in_dim(
        first_state, k_zero + place % 4 * second_width, second_width, 1
    )
    second_term = jnp.dot(second_piece, up_two, preferred_element_type=jnp.float32)
    second_sum = sum_sixteen(second_term)
    second_state = second_sum.astype(jnp.bfloat16)
    root_piece = lax.dynamic_slice_in_dim(
        second_state, k_one + place % 16 * root_width, root_width, 1
    )
    root_term = jnp.dot(root_piece, up_root, preferred_element_type=jnp.float32)
    root_state = lax.psum(root_term, ("gx", "gy")).astype(jnp.bfloat16)
    top_piece = contract(root_state, down_root).astype(jnp.bfloat16)
    top_bound = join_sixteen(top_piece, place)
    second_input = jnp.concatenate([second_state[:, :k_one], top_bound], axis=1)
    mid_piece = contract(second_input, down_two).astype(jnp.bfloat16)
    mid_bound = mid_piece
    for bit_num in range(2):
        other = partner(mid_bound, "gy", bit_num)
        mid_bound = place_pair(mid_bound, other, place, bit_num)
    first_input = jnp.concatenate([first_state[:, :k_zero], mid_bound], axis=1)
    box_bound = contract(first_input, down_one).astype(jnp.bfloat16)
    box_input = jnp.concatenate([box_state[:, :inner_dev], box_bound], axis=1)
    leaf_bound = (
        contract(box_input, box_down).astype(jnp.bfloat16).reshape(rhs_count, leaves, edge_count)
    )
    lifted = jnp.einsum(
        "rle,leq->rlq",
        leaf_bound,
        leaf_lift.reshape(leaves, edge_count, points),
        preferred_element_type=jnp.float32,
    )
    particular = jnp.einsum(
        "rlq,lqp->rlp",
        source,
        leaf_particular.reshape(leaves, points, points),
        preferred_element_type=jnp.float32,
    )
    return lifted + particular


def solution(mesh):
    return jax.shard_map(
        per_device,
        mesh=mesh,
        in_specs=(
            P(None, ("gx", "gy"), None),
            P(("gx", "gy"), None),
            P(("gx", "gy"), None),
            P(("gx", "gy"), None),
            P(("gx", "gy"), None),
            P(("gx", "gy"), None),
            P(("gx", "gy"), None),
            P(("gx", "gy"), None),
            P(("gx", "gy"), None),
            P(("gx", "gy"), None),
            P(("gx", "gy"), None),
            P(("gx", "gy"), None),
        ),
        out_specs=P(None, ("gx", "gy"), None),
        check_vma=False,
    )
```

profile of v0, /device:TPU:6, one launch (start us, length us, event | category | flops | bytes accessed | tf_op | source)
XLA Modules:
  0.0 143.0 jit_solution(12066938558323043604)
XLA Ops:
  0.0 1.4 %fusion.1 = bf16[16,16,64]{2,0,1:T(8,128)(2,1)S(1)} fusion(bf16[16,64,256]{2,1,0:T(8,128)(2,1)} %bitcast.25, bf16[16,16,256]{2,1,0:T(8,128)(2,1)} %param.12), kind=kOutput, calls=%fused_computation.4 | convolution fusion | flops 8404992 | bytes 688128 | tf_op jit(solution)/shard_map/rlq,leq->rle/dot_general | solution.py:64
  1.6 1.8 %convolution_convert_fusion.2 = bf16[16,640]{1,0:T(8,128)(2,1)S(1)} fusion(bf16[16,1024]{1,0:T(8,128)(2,1)S(1)} %reshape.16, bf16[640,1024]{1,0:T(8,128)(2,1)} %param.16), kind=kOutput, calls=%fused_computation.6 | convolution fusion | flops 20981760 | bytes 1363968 | tf_op jit(solution)/shard_map/dot_general | solution.py:12
  3.4 0.2 fusion.34
  3.6 1.6 %collective-permute-start = (bf16[16,768]{1,0:T(8,128)(2,1)S(1)}, bf16[16,768]{1,0:T(8,128)(2,1)S(1)}, u32[]{:S(2)}, u32[]{:S(2)}) collective-permute-start(bf16[16,768]{1,0:T(8,128)(2,1)S(1)} %get-tuple-element.17), channel_id=1, source_target_pairs={{0,1},{1,0},{2,3},{3,2},{4,5},{5,4},{6,7},{7,6},{8,9},{9,8},{10,11... | collective-permute-start | bytes 73736 | tf_op jit(solution)/shard_map/ppermute | solution.py:8
  5.3 2.2 %collective-permute-done = bf16[16,768]{1,0:T(8,128)(2,1)S(1)} collective-permute-done((bf16[16,768]{1,0:T(8,128)(2,1)S(1)}, bf16[16,768]{1,0:T(8,128)(2,1)S(1)}, u32[]{:S(2)}, u32[]{:S(2)}) %collective-permute-start) | collective-permute-done | bytes 24608 | tf_op jit(solution)/shard_map/ppermute | solution.py:8
  7.5 3.3 %collective-permute-start.1 = (bf16[16,768]{1,0:T(8,128)(2,1)S(1)}, bf16[16,768]{1,0:T(8,128)(2,1)S(1)}, u32[]{:S(2)}, u32[]{:S(2)}) collective-permute-start(bf16[16,768]{1,0:T(8,128)(2,1)S(1)} %fusion.13), channel_id=1, source_target_pairs={{0,2},{1,3},{2,0},{3,1},{4,6},{5,7},{6,4},{7,5},{8,10},{9,11},{10,... | collective-permute-start | bytes 73736 | tf_op jit(solution)/shard_map/ppermute | solution.py:8
  10.8 2.1 %collective-permute-done.1 = bf16[16,768]{1,0:T(8,128)(2,1)S(1)} collective-permute-done((bf16[16,768]{1,0:T(8,128)(2,1)S(1)}, bf16[16,768]{1,0:T(8,128)(2,1)S(1)}, u32[]{:S(2)}, u32[]{:S(2)}) %collective-permute-start.1) | collective-permute-done | bytes 24608 | tf_op jit(solution)/shard_map/ppermute | solution.py:8
  13.1 1.7 %collective-permute-start.2 = (bf16[16,1536]{1,0:T(8,128)(2,1)S(1)}, bf16[16,1536]{1,0:T(8,128)(2,1)S(1)}, u32[]{:S(2)}, u32[]{:S(2)}) collective-permute-start(bf16[16,1536]{1,0:T(8,128)(2,1)S(1)} %get-tuple-element.19), channel_id=1, source_target_pairs={{0,1},{1,0},{2,3},{3,2},{4,5},{5,4},{6,7},{7,6},{8,9},{9,8},{10,11... | collective-permute-start | bytes 147464 | tf_op jit(solution)/shard_map/ppermute | solution.py:8
  14.8 2.5 %collective-permute-done.2 = bf16[16,1536]{1,0:T(8,128)(2,1)S(1)} collective-permute-done((bf16[16,1536]{1,0:T(8,128)(2,1)S(1)}, bf16[16,1536]{1,0:T(8,128)(2,1)S(1)}, u32[]{:S(2)}, u32[]{:S(2)}) %collective-permute-start.2) | collective-permute-done | bytes 49184 | tf_op jit(solution)/shard_map/ppermute | solution.py:8
  17.3 3.7 %collective-permute-start.3 = (bf16[16,1536]{1,0:T(8,128)(2,1)S(1)}, bf16[16,1536]{1,0:T(8,128)(2,1)S(1)}, u32[]{:S(2)}, u32[]{:S(2)}) collective-permute-start(bf16[16,1536]{1,0:T(8,128)(2,1)S(1)} %fusion.5), channel_id=1, source_target_pairs={{0,2},{1,3},{2,0},{3,1},{4,6},{5,7},{6,4},{7,5},{8,10},{9,11},{10,... | collective-permute-start | bytes 147464 | tf_op jit(solution)/shard_map/ppermute | solution.py:8
  21.0 2.1 %collective-permute-done.3 = bf16[16,1536]{1,0:T(8,128)(2,1)S(1)} collective-permute-done((bf16[16,1536]{1,0:T(8,128)(2,1)S(1)}, bf16[16,1536]{1,0:T(8,128)(2,1)S(1)}, u32[]{:S(2)}, u32[]{:S(2)}) %collective-permute-start.3) | collective-permute-done | bytes 49184 | tf_op jit(solution)/shard_map/ppermute | solution.py:8
  23.1 2.0 %collective-permute-start.4 = (bf16[16,1536]{1,0:T(8,128)(2,1)S(1)}, bf16[16,1536]{1,0:T(8,128)(2,1)S(1)}, u32[]{:S(2)}, u32[]{:S(2)}) collective-permute-start(bf16[16,1536]{1,0:T(8,128)(2,1)S(1)} %fusion.33), channel_id=1, source_target_pairs={{0,4},{1,5},{2,6},{3,7},{4,0},{5,1},{6,2},{7,3},{8,12},{9,13},{10,... | collective-permute-start | bytes 147464 | tf_op jit(solution)/shard_map/ppermute | solution.py:8
  25.1 2.2 %collective-permute-done.4 = bf16[16,1536]{1,0:T(8,128)(2,1)S(1)} collective-permute-done((bf16[16,1536]{1,0:T(8,128)(2,1)S(1)}, bf16[16,1536]{1,0:T(8,128)(2,1)S(1)}, u32[]{:S(2)}, u32[]{:S(2)}) %collective-permute-start.4) | collective-permute-done | bytes 49184 | tf_op jit(solution)/shard_map/ppermute | solution.py:8
  27.3 3.4 %collective-permute-start.5 = (bf16[16,1536]{1,0:T(8,128)(2,1)S(1)}, bf16[16,1536]{1,0:T(8,128)(2,1)S(1)}, u32[]{:S(2)}, u32[]{:S(2)}) collective-permute-start(bf16[16,1536]{1,0:T(8,128)(2,1)S(1)} %fusion.6), channel_id=1, source_target_pairs={{0,8},{1,9},{2,10},{3,11},{4,12},{5,13},{6,14},{7,15},{8,0},{9,1},... | collective-permute-start | bytes 147464 | tf_op jit(solution)/shard_map/ppermute | solution.py:8
  30.7 2.1 %collective-permute-done.5 = bf16[16,1536]{1,0:T(8,128)(2,1)S(1)} collective-permute-done((bf16[16,1536]{1,0:T(8,128)(2,1)S(1)}, bf16[16,1536]{1,0:T(8,128)(2,1)S(1)}, u32[]{:S(2)}, u32[]{:S(2)}) %collective-permute-start.5) | collective-permute-done | bytes 49184 | tf_op jit(solution)/shard_map/ppermute | solution.py:8
  32.8 0.3 fusion.24
  33.1 80.1 %all-reduce.1 = bf16[16,6144]{1,0:T(8,128)(2,1)S(1)} all-reduce(f32[16,6144]{1,0:T(8,128)S(1)} %fusion.24), channel_id=1, replica_groups=mesh['gx'=8,'gy'=32] {'gx','gy'}, use_global_device_ids=true, to_apply=%region_0.1 | all-reduce | flops 98304 | bytes 589824 | tf_op jit(solution)/shard_map/psum | solution.py:90
  113.2 1.4 %convolution_convert_fusion.4 = bf16[16,64]{1,0:T(8,128)(2,1)S(1)} fusion(bf16[64,6144]{1,0:T(8,128)(2,1)} %param.23, bf16[16,6144]{1,0:T(8,128)(2,1)S(1)} %all-reduce.1), kind=kOutput, calls=%fused_computation.8 | convolution fusion | flops 12583936 | bytes 985088 | tf_op jit(solution)/shard_map/dot_general | solution.py:12
  114.7 3.6 %collective-permute-done.6 = bf16[16,64]{1,0:T(8,128)(2,1)S(1)} collective-permute-done((bf16[16,64]{1,0:T(8,128)(2,1)S(1)}, bf16[16,64]{1,0:T(8,128)(2,1)S(1)}, u32[]{:S(2)}, u32[]{:S(2)}) %collective-permute-start.6) | collective-permute-done | bytes 2080 | tf_op jit(solution)/shard_map/ppermute | solution.py:8
  118.4 0.9 collective-permute-start.7
  119.2 4.3 %collective-permute-done.7 = bf16[16,128]{1,0:T(8,128)(2,1)S(1)} collective-permute-done((bf16[16,128]{1,0:T(8,128)(2,1)S(1)}, bf16[16,128]{1,0:T(8,128)(2,1)S(1)}, u32[]{:S(2)}, u32[]{:S(2)}) %collective-permute-start.7) | collective-permute-done | bytes 4128 | tf_op jit(solution)/shard_map/ppermute | solution.py:8
  123.6 1.1 collective-permute-start.8
  124.7 2.6 %collective-permute-done.8 = bf16[16,256]{1,0:T(8,128)(2,1)S(1)} collective-permute-done((bf16[16,256]{1,0:T(8,128)(2,1)S(1)}, bf16[16,256]{1,0:T(8,128)(2,1)S(1)}, u32[]{:S(2)}, u32[]{:S(2)}) %collective-permute-start.8) | collective-permute-done | bytes 8224 | tf_op jit(solution)/shard_map/ppermute | solution.py:8
  127.3 0.5 collective-permute-start.9
  127.8 4.2 %collective-permute-done.9 = bf16[16,512]{1,0:T(8,128)(2,1)S(1)} collective-permute-done((bf16[16,512]{1,0:T(8,128)(2,1)S(1)}, bf16[16,512]{1,0:T(8,128)(2,1)S(1)}, u32[]{:S(2)}, u32[]{:S(2)}) %collective-permute-start.9) | collective-permute-done | bytes 16416 | tf_op jit(solution)/shard_map/ppermute | solution.py:8
  132.0 0.2 convolution_convert_fusion.5
  132.2 3.6 %collective-permute-done.10 = bf16[16,128]{1,0:T(8,128)(2,1)S(1)} collective-permute-done((bf16[16,128]{1,0:T(8,128)(2,1)S(1)}, bf16[16,128]{1,0:T(8,128)(2,1)S(1)}, u32[]{:S(2)}, u32[]{:S(2)}) %collective-permute-start.10) | collective-permute-done | bytes 4128 | tf_op jit(solution)/shard_map/ppermute | solution.py:8
  135.9 1.0 collective-permute-start.11
  136.8 0.4 convolution_bitcast_fusion.1
  137.2 3.9 %collective-permute-done.11 = bf16[16,256]{1,0:T(8,128)(2,1)S(1)} collective-permute-done((bf16[16,256]{1,0:T(8,128)(2,1)S(1)}, bf16[16,256]{1,0:T(8,128)(2,1)S(1)}, u32[]{:S(2)}, u32[]{:S(2)}) %collective-permute-start.11) | collective-permute-done | bytes 8224 | tf_op jit(solution)/shard_map/ppermute | solution.py:8
  141.3 0.5 convolution_convert_fusion.1
  142.1 0.9 copy.21
  (45 shorter events, 1.2 us)
Async XLA Ops:
  0.0 136.8 %copy-start = (bf16[4096,256]{1,0:T(8,128)(2,1)S(1)}, bf16[4096,256]{1,0:T(8,128)(2,1)}, u32[]{:S(2)}) copy-start(bf16[4096,256]{1,0:T(8,128)(2,1)} %param.14) | copy-start | bytes 6291460
  1.4 11.5 %copy-start.5 = (bf16[128,1536]{1,0:T(8,128)(2,1)S(1)}, bf16[128,1536]{1,0:T(8,128)(2,1)}, u32[]{:S(2)}) copy-start(bf16[128,1536]{1,0:T(8,128)(2,1)} %param.20) | copy-start | bytes 1179652
  1.6 1.8 %copy-start.8 = (bf16[256,768]{1,0:T(8,128)(2,1)S(1)}, bf16[256,768]{1,0:T(8,128)(2,1)}, u32[]{:S(2)}) copy-start(bf16[256,768]{1,0:T(8,128)(2,1)} %param.18) | copy-start | bytes 1179652
  3.4 29.4 %copy-start.2 = (bf16[64,6144]{1,0:T(8,128)(2,1)S(1)}, bf16[64,6144]{1,0:T(8,128)(2,1)}, u32[]{:S(2)}) copy-start(bf16[64,6144]{1,0:T(8,128)(2,1)} %param.22) | copy-start | bytes 2359300
  3.6 3.9 %collective-permute-start = (bf16[16,768]{1,0:T(8,128)(2,1)S(1)}, bf16[16,768]{1,0:T(8,128)(2,1)S(1)}, u32[]{:S(2)}, u32[]{:S(2)}) collective-permute-start(bf16[16,768]{1,0:T(8,128)(2,1)S(1)} %get-tuple-element.17), channel_id=1, source_target_pairs={{0,1},{1,0},{2,3},{3,2},{4,5},{5,4},{6,7},{7,6},{8,9},{9,8},{10,11... | collective-permute-start | bytes 73736 | tf_op jit(solution)/shard_map/ppermute | solution.py:8
  7.5 5.4 %collective-permute-start.1 = (bf16[16,768]{1,0:T(8,128)(2,1)S(1)}, bf16[16,768]{1,0:T(8,128)(2,1)S(1)}, u32[]{:S(2)}, u32[]{:S(2)}) collective-permute-start(bf16[16,768]{1,0:T(8,128)(2,1)S(1)} %fusion.13), channel_id=1, source_target_pairs={{0,2},{1,3},{2,0},{3,1},{4,6},{5,7},{6,4},{7,5},{8,10},{9,11},{10,... | collective-permute-start | bytes 73736 | tf_op jit(solution)/shard_map/ppermute | solution.py:8
  13.1 4.2 %collective-permute-start.2 = (bf16[16,1536]{1,0:T(8,128)(2,1)S(1)}, bf16[16,1536]{1,0:T(8,128)(2,1)S(1)}, u32[]{:S(2)}, u32[]{:S(2)}) collective-permute-start(bf16[16,1536]{1,0:T(8,128)(2,1)S(1)} %get-tuple-element.19), channel_id=1, source_target_pairs={{0,1},{1,0},{2,3},{3,2},{4,5},{5,4},{6,7},{7,6},{8,9},{9,8},{10,11... | collective-permute-start | bytes 147464 | tf_op jit(solution)/shard_map/ppermute | solution.py:8
  17.3 5.8 %collective-permute-start.3 = (bf16[16,1536]{1,0:T(8,128)(2,1)S(1)}, bf16[16,1536]{1,0:T(8,128)(2,1)S(1)}, u32[]{:S(2)}, u32[]{:S(2)}) collective-permute-start(bf16[16,1536]{1,0:T(8,128)(2,1)S(1)} %fusion.5), channel_id=1, source_target_pairs={{0,2},{1,3},{2,0},{3,1},{4,6},{5,7},{6,4},{7,5},{8,10},{9,11},{10,... | collective-permute-start | bytes 147464 | tf_op jit(solution)/shard_map/ppermute | solution.py:8
  23.1 4.2 %collective-permute-start.4 = (bf16[16,1536]{1,0:T(8,128)(2,1)S(1)}, bf16[16,1536]{1,0:T(8,128)(2,1)S(1)}, u32[]{:S(2)}, u32[]{:S(2)}) collective-permute-start(bf16[16,1536]{1,0:T(8,128)(2,1)S(1)} %fusion.33), channel_id=1, source_target_pairs={{0,4},{1,5},{2,6},{3,7},{4,0},{5,1},{6,2},{7,3},{8,12},{9,13},{10,... | collective-permute-start | bytes 147464 | tf_op jit(solution)/shard_map/ppermute | solution.py:8
  27.3 5.4 %collective-permute-start.5 = (bf16[16,1536]{1,0:T(8,128)(2,1)S(1)}, bf16[16,1536]{1,0:T(8,128)(2,1)S(1)}, u32[]{:S(2)}, u32[]{:S(2)}) collective-permute-start(bf16[16,1536]{1,0:T(8,128)(2,1)S(1)} %fusion.6), channel_id=1, source_target_pairs={{0,8},{1,9},{2,10},{3,11},{4,12},{5,13},{6,14},{7,15},{8,0},{9,1},... | collective-permute-start | bytes 147464 | tf_op jit(solution)/shard_map/ppermute | solution.py:8
  33.1 98.9 %copy-start.6 = (bf16[128,1536]{1,0:T(8,128)(2,1)S(1)}, bf16[128,1536]{1,0:T(8,128)(2,1)}, u32[]{:S(2)}) copy-start(bf16[128,1536]{1,0:T(8,128)(2,1)} %param.21) | copy-start | bytes 1179652
  33.1 103.7 %copy-start.4 = (bf16[16,16,256]{2,1,0:T(8,128)(2,1)S(1)}, bf16[16,16,256]{2,1,0:T(8,128)(2,1)}, u32[]{:S(2)}) copy-start(bf16[16,16,256]{2,1,0:T(8,128)(2,1)} %param.12) | copy-start | bytes 393220
  114.6 3.6 %collective-permute-start.6 = (bf16[16,64]{1,0:T(8,128)(2,1)S(1)}, bf16[16,64]{1,0:T(8,128)(2,1)S(1)}, u32[]{:S(2)}, u32[]{:S(2)}) collective-permute-start(bf16[16,64]{1,0:T(8,128)(2,1)S(1)} %convolution_convert_fusion.4), channel_id=1, source_target_pairs={{0,1},{1,0},{2,3},{3,2},{4,5},{5,4},{6,7},{7,6},{8,9},{9,8},{10,11... | collective-permute-start | bytes 6152 | tf_op jit(solution)/shard_map/ppermute | solution.py:8
  118.4 5.1 %collective-permute-start.7 = (bf16[16,128]{1,0:T(8,128)(2,1)S(1)}, bf16[16,128]{1,0:T(8,128)(2,1)S(1)}, u32[]{:S(2)}, u32[]{:S(2)}) collective-permute-start(bf16[16,128]{1,0:T(8,128)(2,1)S(1)} %pad_maximum_fusion.3), channel_id=1, source_target_pairs={{0,2},{1,3},{2,0},{3,1},{4,6},{5,7},{6,4},{7,5},{8,10},{9,11},{10,... | collective-permute-start | bytes 12296 | tf_op jit(solution)/shard_map/ppermute | solution.py:8
  123.6 3.7 %collective-permute-start.8 = (bf16[16,256]{1,0:T(8,128)(2,1)S(1)}, bf16[16,256]{1,0:T(8,128)(2,1)S(1)}, u32[]{:S(2)}, u32[]{:S(2)}) collective-permute-start(bf16[16,256]{1,0:T(8,128)(2,1)S(1)} %pad_maximum_fusion.1), channel_id=1, source_target_pairs={{0,4},{1,5},{2,6},{3,7},{4,0},{5,1},{6,2},{7,3},{8,12},{9,13},{10,... | collective-permute-start | bytes 24584 | tf_op jit(solution)/shard_map/ppermute | solution.py:8
  127.3 4.7 %collective-permute-start.9 = (bf16[16,512]{1,0:T(8,128)(2,1)S(1)}, bf16[16,512]{1,0:T(8,128)(2,1)S(1)}, u32[]{:S(2)}, u32[]{:S(2)}) collective-permute-start(bf16[16,512]{1,0:T(8,128)(2,1)S(1)} %pad_maximum_fusion), channel_id=1, source_target_pairs={{0,8},{1,9},{2,10},{3,11},{4,12},{5,13},{6,14},{7,15},{8,0},{9,1},... | collective-permute-start | bytes 49160 | tf_op jit(solution)/shard_map/ppermute | solution.py:8
  132.2 8.9 %copy-start.7 = (bf16[256,768]{1,0:T(8,128)(2,1)S(1)}, bf16[256,768]{1,0:T(8,128)(2,1)}, u32[]{:S(2)}) copy-start(bf16[256,768]{1,0:T(8,128)(2,1)} %param.19) | copy-start | bytes 1179652
  132.2 3.6 %collective-permute-start.10 = (bf16[16,128]{1,0:T(8,128)(2,1)S(1)}, bf16[16,128]{1,0:T(8,128)(2,1)S(1)}, u32[]{:S(2)}, u32[]{:S(2)}) collective-permute-start(bf16[16,128]{1,0:T(8,128)(2,1)S(1)} %convolution_convert_fusion.5), channel_id=1, source_target_pairs={{0,1},{1,0},{2,3},{3,2},{4,5},{5,4},{6,7},{7,6},{8,9},{9,8},{10,11... | collective-permute-start | bytes 12296 | tf_op jit(solution)/shard_map/ppermute | solution.py:8
  135.9 5.2 %collective-permute-start.11 = (bf16[16,256]{1,0:T(8,128)(2,1)S(1)}, bf16[16,256]{1,0:T(8,128)(2,1)S(1)}, u32[]{:S(2)}, u32[]{:S(2)}) collective-permute-start(bf16[16,256]{1,0:T(8,128)(2,1)S(1)} %pad_maximum_fusion.2), channel_id=1, source_target_pairs={{0,2},{1,3},{2,0},{3,1},{4,6},{5,7},{6,4},{7,5},{8,10},{9,11},{10,... | collective-permute-start | bytes 24584 | tf_op jit(solution)/shard_map/ppermute | solution.py:8
  136.8 4.5 %copy-start.1 = (bf16[1024,640]{1,0:T(8,128)(2,1)S(1)}, bf16[1024,640]{1,0:T(8,128)(2,1)}, u32[]{:S(2)}) copy-start(bf16[1024,640]{1,0:T(8,128)(2,1)} %param.17) | copy-start | bytes 3932164
  137.2 4.7 %copy-start.3 = (bf16[1024,256]{1,0:T(8,128)(2,1)S(1)}, bf16[1024,256]{1,0:T(8,128)(2,1)}, u32[]{:S(2)}) copy-start(bf16[1024,256]{1,0:T(8,128)(2,1)} %param.15) | copy-start | bytes 1572868
where the time goes:
time: 143 us
  blocking collectives  80.1 us (56%)
  waiting for transfers between devices  35.3 us (25%)
  starting transfers between devices  19.1 us (13%)
  matrix products  6.77 us (5%)
    psum x1, blocking collectives, per_device(): root_state = lax.psum(root_term, ('gx', 'gy')).astype(jnp.bfloat16)  80.1 us
    ppermute x12, waiting for transfers between devices, partner(): lax.ppermute(x, axis, [(i, i ^ 1 << stride) for i in range(lax.axis_size(...  35.3 us
    ppermute x12, starting transfers between devices, partner(): lax.ppermute(x, axis, [(i, i ^ 1 << stride) for i in range(lax.axis_size(...  19.1 us
    dot_general x5, matrix products, contract(): lax.dot_general(left, right, (((1,), (1,)), ((), ())), preferred_element_...  4.13 us
  transfers between devices with their start and end apart: 12, of which 12 were waited for; matrix products, arithmetic and copies ran while one was open for 0% of the time, Pallas kernels for 0%

commit v1 on v0

--- a/solution.py
+++ b/solution.py
@@ -87,7 +87,7 @@
         second_state, k_one + place % 16 * root_width, root_width, 1
     )
     root_term = jnp.dot(root_piece, up_root, preferred_element_type=jnp.float32)
-    root_state = lax.psum(root_term, ("gx", "gy")).astype(jnp.bfloat16)
+    root_state = lax.psum(lax.psum(root_term, "gy"), "gx").astype(jnp.bfloat16)
     top_piece = contract(root_state, down_root).astype(jnp.bfloat16)
     top_bound = join_sixteen(top_piece, place)
     second_input = jnp.concatenate([second_state[:, :k_one], top_bound], axis=1)

time: 143 us -> 254 us (1.78)
  waiting for transfers between devices: 35.3 us -> 183 us
  blocking collectives: 80.1 us -> 25.1 us
  between operations: 0.16 us -> 13.5 us
  starting transfers between devices: 19.1 us -> 21.9 us
    psum x0 -> x1, waiting for transfers between devices: none -> 150 us  [per_device(): root_state = lax.psum(lax.psum(root_term, 'gy'), 'gx').astype(jnp.bfloat16)]
    psum x1, blocking collectives: 80.1 us -> 25.1 us  [per_device(): root_state = lax.psum(lax.psum(root_term, 'gy'), 'gx').astype(jnp.bfloat16)]
    ppermute x12, starting transfers between devices: 19.1 us -> 21.9 us  [partner(): lax.ppermute(x, axis, [(i, i ^ 1 << stride) for i in range(lax.axis_size(...]
    ppermute x12, waiting for transfers between devices: 35.3 us -> 32.6 us  [partner(): lax.ppermute(x, axis, [(i, i ^ 1 << stride) for i in range(lax.axis_size(...]
  transfers between devices with their start and end apart: 12 -> 13, of which waited for: 12 -> 13; matrix products, arithmetic and copies ran while one was open for 0% -> 0% of each run, Pallas kernels for 0% -> 0%
where the time goes in v1:
time: 254 us; the launch traced here: 252 us
  waiting for transfers between devices  183 us (72%)
  blocking collectives  25.1 us (10%)
  starting transfers between devices  21.9 us (9%)
  between operations  13.5 us (5%)
  matrix products  7.52 us (3%)
    psum x1, waiting for transfers between devices, per_device(): root_state = lax.psum(lax.psum(root_term, 'gy'), 'gx').astype(jnp.bfloat16)  150 us
    ppermute x12, waiting for transfers between devices, partner(): lax.ppermute(x, axis, [(i, i ^ 1 << stride) for i in range(lax.axis_size(...  32.6 us
    psum x1, blocking collectives, per_device(): root_state = lax.psum(lax.psum(root_term, 'gy'), 'gx').astype(jnp.bfloat16)  25.1 us
    ppermute x12, starting transfers between devices, partner(): lax.ppermute(x, axis, [(i, i ^ 1 << stride) for i in range(lax.axis_size(...  21.9 us
  transfers between devices with their start and end apart: 13, of which 13 were waited for; matrix products, arithmetic and copies ran while one was open for 0% of the time, Pallas kernels for 0%

profile of v1, /device:TPU:6, one launch (start us, length us, event | category | flops | bytes accessed | tf_op | source)
XLA Modules:
  0.0 252.1 jit_solution(9659060223524549372)
XLA Ops:
  6.5 1.4 fusion.1
  8.2 1.8 convolution_convert_fusion.2
  10.2 1.6 collective-permute-start
  11.8 2.2 collective-permute-done
  14.1 3.3 %collective-permute-start.1 = (bf16[16,768]{1,0:T(8,128)(2,1)S(1)}, bf16[16,768]{1,0:T(8,128)(2,1)S(1)}, u32[]{:S(2)}, u32[]{:S(2)}) collective-permute-start(bf16[16,768]{1,0:T(8,128)(2,1)S(1)} %fusion.13), channel_id=1, source_target_pairs={{0,2},{1,3},{2,0},{3,1},{4,6},{5,7},{6,4},{7,5},{8,10},{9,11},{10,... | collective-permute-start | bytes 73736 | tf_op jit(solution)/shard_map/ppermute | solution.py:8
  17.3 2.1 collective-permute-done.1
  19.7 1.7 collective-permute-start.2
  21.3 2.5 collective-permute-done.2
  23.8 3.7 %collective-permute-start.3 = (bf16[16,1536]{1,0:T(8,128)(2,1)S(1)}, bf16[16,1536]{1,0:T(8,128)(2,1)S(1)}, u32[]{:S(2)}, u32[]{:S(2)}) collective-permute-start(bf16[16,1536]{1,0:T(8,128)(2,1)S(1)} %fusion.5), channel_id=1, source_target_pairs={{0,2},{1,3},{2,0},{3,1},{4,6},{5,7},{6,4},{7,5},{8,10},{9,11},{10,... | collective-permute-start | bytes 147464 | tf_op jit(solution)/shard_map/ppermute | solution.py:8
  27.6 2.1 collective-permute-done.3
  29.6 2.0 collective-permute-start.4
  31.6 2.2 collective-permute-done.4
  33.8 3.4 %collective-permute-start.5 = (bf16[16,1536]{1,0:T(8,128)(2,1)S(1)}, bf16[16,1536]{1,0:T(8,128)(2,1)S(1)}, u32[]{:S(2)}, u32[]{:S(2)}) collective-permute-start(bf16[16,1536]{1,0:T(8,128)(2,1)S(1)} %fusion.6), channel_id=1, source_target_pairs={{0,8},{1,9},{2,10},{3,11},{4,12},{5,13},{6,14},{7,15},{8,0},{9,1},... | collective-permute-start | bytes 147464 | tf_op jit(solution)/shard_map/ppermute | solution.py:8
  37.2 2.1 collective-permute-done.5
  39.3 1.0 fusion.24
  40.4 149.9 %all-reduce.3.cloned.1.call-done = f32[16,6144]{1,0:T(8,128)} async-done(((f32[16,6144]{1,0:T(8,128)}), f32[16,6144]{1,0:T(8,128)}) %all-reduce.3.cloned.1.call-update) | async-done | bytes 393232 | tf_op jit(solution)/shard_map/psum | solution.py:90
  190.3 25.1 %all-reduce.4 = bf16[16,6144]{1,0:T(8,128)(2,1)S(1)} all-reduce(f32[16,6144]{1,0:T(8,128)} %all-reduce.3.cloned.1.call-done), channel_id=1, replica_groups=mesh['gx'=8,'gy'=32] {'gx'}, use_global_device_ids=true, to_apply=%region_1.2 | all-reduce | flops 98304 | bytes 589824 | tf_op jit(solution)/shard_map/psum | solution.py:90
  215.4 1.4 convolution_convert_fusion.4
  217.1 3.4 %collective-permute-done.6 = bf16[16,64]{1,0:T(8,128)(2,1)S(1)} collective-permute-done((bf16[16,64]{1,0:T(8,128)(2,1)S(1)}, bf16[16,64]{1,0:T(8,128)(2,1)S(1)}, u32[]{:S(2)}, u32[]{:S(2)}) %collective-permute-start.6) | collective-permute-done | bytes 2080 | tf_op jit(solution)/shard_map/ppermute | solution.py:8
  220.6 1.5 collective-permute-start.7
  222.1 3.6 %collective-permute-done.7 = bf16[16,128]{1,0:T(8,128)(2,1)S(1)} collective-permute-done((bf16[16,128]{1,0:T(8,128)(2,1)S(1)}, bf16[16,128]{1,0:T(8,128)(2,1)S(1)}, u32[]{:S(2)}, u32[]{:S(2)}) %collective-permute-start.7) | collective-permute-done | bytes 4128 | tf_op jit(solution)/shard_map/ppermute | solution.py:8
  225.8 0.7 collective-permute-start.8
  226.5 3.0 %collective-permute-done.8 = bf16[16,256]{1,0:T(8,128)(2,1)S(1)} collective-permute-done((bf16[16,256]{1,0:T(8,128)(2,1)S(1)}, bf16[16,256]{1,0:T(8,128)(2,1)S(1)}, u32[]{:S(2)}, u32[]{:S(2)}) %collective-permute-start.8) | collective-permute-done | bytes 8224 | tf_op jit(solution)/shard_map/ppermute | solution.py:8
  229.5 2.0 collective-permute-start.9
  231.5 2.7 %collective-permute-done.9 = bf16[16,512]{1,0:T(8,128)(2,1)S(1)} collective-permute-done((bf16[16,512]{1,0:T(8,128)(2,1)S(1)}, bf16[16,512]{1,0:T(8,128)(2,1)S(1)}, u32[]{:S(2)}, u32[]{:S(2)}) %collective-permute-start.9) | collective-permute-done | bytes 16416 | tf_op jit(solution)/shard_map/ppermute | solution.py:8
  234.4 0.2 collective-permute-start.10
  234.7 3.4 %collective-permute-done.10 = bf16[16,128]{1,0:T(8,128)(2,1)S(1)} collective-permute-done((bf16[16,128]{1,0:T(8,128)(2,1)S(1)}, bf16[16,128]{1,0:T(8,128)(2,1)S(1)}, u32[]{:S(2)}, u32[]{:S(2)}) %collective-permute-start.10) | collective-permute-done | bytes 4128 | tf_op jit(solution)/shard_map/ppermute | solution.py:8
  238.1 1.5 collective-permute-start.11
  239.6 0.4 convolution_bitcast_fusion.1
  240.0 3.3 %collective-permute-done.11 = bf16[16,256]{1,0:T(8,128)(2,1)S(1)} collective-permute-done((bf16[16,256]{1,0:T(8,128)(2,1)S(1)}, bf16[16,256]{1,0:T(8,128)(2,1)S(1)}, u32[]{:S(2)}, u32[]{:S(2)}) %collective-permute-start.11) | collective-permute-done | bytes 8224 | tf_op jit(solution)/shard_map/ppermute | solution.py:8
  243.5 0.5 convolution_convert_fusion.1
  244.4 0.9 copy.21
  (48 shorter events, 1.8 us)
Async XLA Ops:
  6.5 233.1 %copy-start = (bf16[4096,256]{1,0:T(8,128)(2,1)S(1)}, bf16[4096,256]{1,0:T(8,128)(2,1)}, u32[]{:S(2)}) copy-start(bf16[4096,256]{1,0:T(8,128)(2,1)} %param.14) | copy-start | bytes 6291460
  6.5 183.8 %all-reduce.3.cloned.1.call-start = ((), (), s32[]{:S(2)}) async-start(), calls=%async_computation | async-start | bytes 786432 | tf_op jit(solution)/shard_map/psum | solution.py:90
  8.0 11.5 %copy-start.5 = (bf16[128,1536]{1,0:T(8,128)(2,1)S(1)}, bf16[128,1536]{1,0:T(8,128)(2,1)}, u32[]{:S(2)}) copy-start(bf16[128,1536]{1,0:T(8,128)(2,1)} %param.20) | copy-start | bytes 1179652
  8.1 1.8 copy-start.8
  10.0 29.4 %copy-start.2 = (bf16[64,6144]{1,0:T(8,128)(2,1)S(1)}, bf16[64,6144]{1,0:T(8,128)(2,1)}, u32[]{:S(2)}) copy-start(bf16[64,6144]{1,0:T(8,128)(2,1)} %param.22) | copy-start | bytes 2359300
  10.2 3.9 %collective-permute-start = (bf16[16,768]{1,0:T(8,128)(2,1)S(1)}, bf16[16,768]{1,0:T(8,128)(2,1)S(1)}, u32[]{:S(2)}, u32[]{:S(2)}) collective-permute-start(bf16[16,768]{1,0:T(8,128)(2,1)S(1)} %get-tuple-element.17), channel_id=1, source_target_pairs={{0,1},{1,0},{2,3},{3,2},{4,5},{5,4},{6,7},{7,6},{8,9},{9,8},{10,11... | collective-permute-start | bytes 73736 | tf_op jit(solution)/shard_map/ppermute | solution.py:8
  14.1 5.4 %collective-permute-start.1 = (bf16[16,768]{1,0:T(8,128)(2,1)S(1)}, bf16[16,768]{1,0:T(8,128)(2,1)S(1)}, u32[]{:S(2)}, u32[]{:S(2)}) collective-permute-start(bf16[16,768]{1,0:T(8,128)(2,1)S(1)} %fusion.13), channel_id=1, source_target_pairs={{0,2},{1,3},{2,0},{3,1},{4,6},{5,7},{6,4},{7,5},{8,10},{9,11},{10,... | collective-permute-start | bytes 73736 | tf_op jit(solution)/shard_map/ppermute | solution.py:8
  19.7 4.2 %collective-permute-start.2 = (bf16[16,1536]{1,0:T(8,128)(2,1)S(1)}, bf16[16,1536]{1,0:T(8,128)(2,1)S(1)}, u32[]{:S(2)}, u32[]{:S(2)}) collective-permute-start(bf16[16,1536]{1,0:T(8,128)(2,1)S(1)} %get-tuple-element.19), channel_id=1, source_target_pairs={{0,1},{1,0},{2,3},{3,2},{4,5},{5,4},{6,7},{7,6},{8,9},{9,8},{10,11... | collective-permute-start | bytes 147464 | tf_op jit(solution)/shard_map/ppermute | solution.py:8
  23.8 5.8 %collective-permute-start.3 = (bf16[16,1536]{1,0:T(8,128)(2,1)S(1)}, bf16[16,1536]{1,0:T(8,128)(2,1)S(1)}, u32[]{:S(2)}, u32[]{:S(2)}) collective-permute-start(bf16[16,1536]{1,0:T(8,128)(2,1)S(1)} %fusion.5), channel_id=1, source_target_pairs={{0,2},{1,3},{2,0},{3,1},{4,6},{5,7},{6,4},{7,5},{8,10},{9,11},{10,... | collective-permute-start | bytes 147464 | tf_op jit(solution)/shard_map/ppermute | solution.py:8
  29.6 4.2 %collective-permute-start.4 = (bf16[16,1536]{1,0:T(8,128)(2,1)S(1)}, bf16[16,1536]{1,0:T(8,128)(2,1)S(1)}, u32[]{:S(2)}, u32[]{:S(2)}) collective-permute-start(bf16[16,1536]{1,0:T(8,128)(2,1)S(1)} %fusion.33), channel_id=1, source_target_pairs={{0,4},{1,5},{2,6},{3,7},{4,0},{5,1},{6,2},{7,3},{8,12},{9,13},{10,... | collective-permute-start | bytes 147464 | tf_op jit(solution)/shard_map/ppermute | solution.py:8
  33.8 5.4 %collective-permute-start.5 = (bf16[16,1536]{1,0:T(8,128)(2,1)S(1)}, bf16[16,1536]{1,0:T(8,128)(2,1)S(1)}, u32[]{:S(2)}, u32[]{:S(2)}) collective-permute-start(bf16[16,1536]{1,0:T(8,128)(2,1)S(1)} %fusion.6), channel_id=1, source_target_pairs={{0,8},{1,9},{2,10},{3,11},{4,12},{5,13},{6,14},{7,15},{8,0},{9,1},... | collective-permute-start | bytes 147464 | tf_op jit(solution)/shard_map/ppermute | solution.py:8
  40.4 193.9 %copy-start.6 = (bf16[128,1536]{1,0:T(8,128)(2,1)S(1)}, bf16[128,1536]{1,0:T(8,128)(2,1)}, u32[]{:S(2)}) copy-start(bf16[128,1536]{1,0:T(8,128)(2,1)} %param.21) | copy-start | bytes 1179652
  40.4 199.3 %copy-start.4 = (bf16[16,16,256]{2,1,0:T(8,128)(2,1)S(1)}, bf16[16,16,256]{2,1,0:T(8,128)(2,1)}, u32[]{:S(2)}) copy-start(bf16[16,16,256]{2,1,0:T(8,128)(2,1)} %param.12) | copy-start | bytes 393220
  216.9 3.6 %collective-permute-start.6 = (bf16[16,64]{1,0:T(8,128)(2,1)S(1)}, bf16[16,64]{1,0:T(8,128)(2,1)S(1)}, u32[]{:S(2)}, u32[]{:S(2)}) collective-permute-start(bf16[16,64]{1,0:T(8,128)(2,1)S(1)} %convolution_convert_fusion.4), channel_id=1, source_target_pairs={{0,1},{1,0},{2,3},{3,2},{4,5},{5,4},{6,7},{7,6},{8,9},{9,8},{10,11... | collective-permute-start | bytes 6152 | tf_op jit(solution)/shard_map/ppermute | solution.py:8
  220.6 5.1 %collective-permute-start.7 = (bf16[16,128]{1,0:T(8,128)(2,1)S(1)}, bf16[16,128]{1,0:T(8,128)(2,1)S(1)}, u32[]{:S(2)}, u32[]{:S(2)}) collective-permute-start(bf16[16,128]{1,0:T(8,128)(2,1)S(1)} %pad_maximum_fusion.3), channel_id=1, source_target_pairs={{0,2},{1,3},{2,0},{3,1},{4,6},{5,7},{6,4},{7,5},{8,10},{9,11},{10,... | collective-permute-start | bytes 12296 | tf_op jit(solution)/shard_map/ppermute | solution.py:8
  225.8 3.7 %collective-permute-start.8 = (bf16[16,256]{1,0:T(8,128)(2,1)S(1)}, bf16[16,256]{1,0:T(8,128)(2,1)S(1)}, u32[]{:S(2)}, u32[]{:S(2)}) collective-permute-start(bf16[16,256]{1,0:T(8,128)(2,1)S(1)} %pad_maximum_fusion.1), channel_id=1, source_target_pairs={{0,4},{1,5},{2,6},{3,7},{4,0},{5,1},{6,2},{7,3},{8,12},{9,13},{10,... | collective-permute-start | bytes 24584 | tf_op jit(solution)/shard_map/ppermute | solution.py:8
  229.5 4.7 %collective-permute-start.9 = (bf16[16,512]{1,0:T(8,128)(2,1)S(1)}, bf16[16,512]{1,0:T(8,128)(2,1)S(1)}, u32[]{:S(2)}, u32[]{:S(2)}) collective-permute-start(bf16[16,512]{1,0:T(8,128)(2,1)S(1)} %pad_maximum_fusion), channel_id=1, source_target_pairs={{0,8},{1,9},{2,10},{3,11},{4,12},{5,13},{6,14},{7,15},{8,0},{9,1},... | collective-permute-start | bytes 49160 | tf_op jit(solution)/shard_map/ppermute | solution.py:8
  234.4 8.9 %copy-start.7 = (bf16[256,768]{1,0:T(8,128)(2,1)S(1)}, bf16[256,768]{1,0:T(8,128)(2,1)}, u32[]{:S(2)}) copy-start(bf16[256,768]{1,0:T(8,128)(2,1)} %param.19) | copy-start | bytes 1179652
  234.4 3.6 %collective-permute-start.10 = (bf16[16,128]{1,0:T(8,128)(2,1)S(1)}, bf16[16,128]{1,0:T(8,128)(2,1)S(1)}, u32[]{:S(2)}, u32[]{:S(2)}) collective-permute-start(bf16[16,128]{1,0:T(8,128)(2,1)S(1)} %convolution_convert_fusion.5), channel_id=1, source_target_pairs={{0,1},{1,0},{2,3},{3,2},{4,5},{5,4},{6,7},{7,6},{8,9},{9,8},{10,11... | collective-permute-start | bytes 12296 | tf_op jit(solution)/shard_map/ppermute | solution.py:8
  238.1 5.2 %collective-permute-start.11 = (bf16[16,256]{1,0:T(8,128)(2,1)S(1)}, bf16[16,256]{1,0:T(8,128)(2,1)S(1)}, u32[]{:S(2)}, u32[]{:S(2)}) collective-permute-start(bf16[16,256]{1,0:T(8,128)(2,1)S(1)} %pad_maximum_fusion.2), channel_id=1, source_target_pairs={{0,2},{1,3},{2,0},{3,1},{4,6},{5,7},{6,4},{7,5},{8,10},{9,11},{10,... | collective-permute-start | bytes 24584 | tf_op jit(solution)/shard_map/ppermute | solution.py:8
  239.6 3.9 %copy-start.1 = (bf16[1024,640]{1,0:T(8,128)(2,1)S(1)}, bf16[1024,640]{1,0:T(8,128)(2,1)}, u32[]{:S(2)}) copy-start(bf16[1024,640]{1,0:T(8,128)(2,1)} %param.17) | copy-start | bytes 3932164
  240.0 4.2 %copy-start.3 = (bf16[1024,256]{1,0:T(8,128)(2,1)S(1)}, bf16[1024,256]{1,0:T(8,128)(2,1)}, u32[]{:S(2)}) copy-start(bf16[1024,256]{1,0:T(8,128)(2,1)} %param.15) | copy-start | bytes 1572868
Sparse Core Ops, SparseCore 0:
  40.5 149.7 all-reduce.2
